TPU v7x, 256 devices: a whole 4x4x8 slice. The times are simulated.
256 devices in a mesh: obs: 4 (over x), bfly: 64 (over z, y, core).
Axes of the slice: x: 4, y: 4, z: 8, core: 2. Of those that a mesh axis runs over, the one named last changes fastest.
Arguments:
- obs_field: float32 [262144, 1024], P(('obs', 'bfly')), may hold values from -6 to 6
- observer_leaf_bases: float32 [512, 512, 256], P(('obs', 'bfly')), may hold values from -0.25 to 0.25
- transfer: float32 [4, 512, 256, 512], P(None, ('obs', 'bfly')), may hold values from -0.25 to 0.25
- src_basis: float32 [128, 512, 256], P('bfly'), may hold values from -0.375 to 0.375
- leaf_map: int32 [4, 64], replicated, may hold values from 0 to 3, as said below
- partner_perm: int32 [4, 256], replicated, may hold values from 0 to 255, each once within a row
Outputs:
- src_field: float32 [1024, 65536], P('obs', 'bfly')
Inputs may be any that keep to these rules, and one draw needn't show every extreme that they name: In every column b, leaf_map[o, b] = (o + r_b) mod 4 for one offset r_b of that column, so each column names every observer group once. `partner_perm`: each row is a permutation of the rank indices.
All inputs are finite; a program needn't handle non-finite values.
Results may differ from a plain program's by a relative error of at most 0.0001.
Values sent between devices are 32-bit elements; how exact they have to be, the bound alone decides.
No kernel may reach another device: no remote copies, remote signals or barrier semaphores. Data moves between devices by JAX's collectives and lax.ppermute only.
A program may use at most 64 MiB of HBM per device.

v0:
```python
import jax
import jax.numpy as jnp
from jax import lax
from jax.sharding import PartitionSpec as P


def swapped(block, axis, apart):
    count = lax.axis_size(axis)
    route = []
    for low in range(count):
        high = low | 1 << apart
        if high != low and high < count:
            route += [(low, high), (high, low)]
    return lax.ppermute(block, axis, route)


def body(obs_field, observer_leaf_bases, transfer, src_basis, leaf_map, partner_perm):
    highest_level = lax.Precision.HIGHEST
    node_count, leaf_rows, rank_size = observer_leaf_bases.shape
    col_count = obs_field.shape[1]
    level_count = transfer.shape[0]
    n_groups = lax.axis_size("obs")
    obs_index = lax.axis_index("obs")
    bfly_index = lax.axis_index("bfly")
    block_list = obs_field.reshape(node_count, leaf_rows, col_count)
    projected_field = jnp.einsum(
        "jlr,jlc->jrc",
        observer_leaf_bases,
        block_list,
        precision=highest_level,
        preferred_element_type=jnp.float32,
    )
    source = leaf_map[obs_index, bfly_index]
    block_rows = node_count * rank_size
    flattened = projected_field.reshape(block_rows, col_count)
    target = source * block_rows
    shards = lax.all_gather(flattened, "obs", axis=0, tiled=True)
    first_row = jnp.int32(0)
    row_count = shards.shape[0]
    offset = jnp.clip(target, 0, row_count - block_rows)
    sliced_rows = lax.dynamic_slice_in_dim(shards, offset, block_rows, 0)
    inside = jnp.logical_and(target >= first_row, target < first_row + row_count)
    gathered = jnp.where(inside, sliced_rows, jnp.zeros_like(flattened))
    carried = gathered.reshape(node_count, rank_size, col_count)
    rank_index_list = jnp.arange(rank_size, dtype=jnp.int32)
    for level_index in range(level_count):
        partner = swapped(carried, "bfly", level_index)
        perm_row = partner_perm[level_index]
        onehot = (perm_row[:, None] == rank_index_list[None, :]).astype(jnp.float32)
        level_mats = transfer[level_index]
        own_part = level_mats[:, :, :rank_size]
        far_part = jnp.einsum(
            "jri,im->jrm",
            level_mats[:, :, rank_size:],
            onehot,
            precision=highest_level,
            preferred_element_type=jnp.float32,
        )
        own_term = jnp.einsum(
            "jrs,jsc->jrc",
            own_part,
            carried,
            precision=highest_level,
            preferred_element_type=jnp.float32,
        )
        far_term = jnp.einsum(
            "jrs,jsc->jrc",
            far_part,
            partner,
            precision=highest_level,
            preferred_element_type=jnp.float32,
        )
        carried = own_term + far_term
    share_cols = col_count // n_groups
    product = jnp.einsum(
        "jlr,jrc->cjl",
        src_basis,
        carried,
        precision=highest_level,
        preferred_element_type=jnp.float32,
    )
    return lax.psum_scatter(
        product.reshape(share_cols * lax.axis_size("obs"), node_count * leaf_rows),
        "obs",
        scatter_dimension=0,
        tiled=True,
    )


def solution(mesh):
    placed = (
        P(("obs", "bfly"), None),
        P(("obs", "bfly"), None, None),
        P(None, ("obs", "bfly"), None, None),
        P("bfly", None, None),
        P(),
        P(),
    )
    return jax.shard_map(
        body, mesh=mesh, in_specs=placed, out_specs=P("obs", "bfly"), check_vma=False
    )
```

profile of v0, /device:TPU:1, one launch (start us, length us, event | category | flops | bytes accessed | tf_op | source)
XLA Modules:
  0.0 332.2 jit_solution(14697301958873001551)
XLA Ops:
  6.5 7.6 %fusion.30 = f32[2,256,1024]{2,1,0:T(8,128)} fusion(f32[2,512,256]{2,1,0:T(8,128)} %param.7, f32[2,512,1024]{2,1,0:T(8,128)} %bitcast.70), kind=kOutput, calls=%fused_computation.43 | convolution fusion | flops 3221225472 | bytes 7340032 | tf_op jit(solution)/shard_map/jlr,jlc->jrc/dot_general | solution.py:26
  14.2 1.3 dynamic_slice.6
  16.1 87.6 %all-gather.2.cloned.1.call-done = f32[2048,1024]{1,0:T(8,128)} async-done(((f32[512,1024]{1,0:T(8,128)}), f32[2048,1024]{1,0:T(8,128)}) %all-gather.2.cloned.1.call-update) | async-done | bytes 8388624 | tf_op jit(solution)/shard_map/all_gather | solution.py:37
  103.7 2.0 dynamic-slice_select_fusion
  105.8 0.9 collective-permute-start
  107.2 0.5 convolution_bitcast_fusion.2
  107.6 3.5 %fusion.12 = f32[2,1024,256]{2,1,0:T(8,128)S(1)} fusion(f32[2,256,1024]{2,1,0:T(8,128)S(1)} %bitcast.69, f32[2,256,512]{2,1,0:T(8,128)S(1)} %get-tuple-element.7), kind=kOutput, calls=%fused_computation.24 | convolution fusion | flops 1610612736 | bytes 4718592 | tf_op jit(solution)/shard_map/jrs,jsc->jrc/dot_general | solution.py:59
  111.1 3.5 %bitcast_add_fusion.4 = f32[2,256,1024]{1,2,0:T(8,128)S(1)} fusion(f32[2,1024,256]{2,1,0:T(8,128)S(1)} %fusion.12, f32[2,256,256]{2,1,0:T(8,128)S(1)} %convolution_bitcast_fusion.2, f32[2,256,1024]{2,1,0:T(8,128)S(1)} %collective-permute-done), kind=kOutput, calls=%fused_computation.4 | convolution fusion | flops 1611137024 | bytes 6815744 | tf_op jit(solution)/shard_map/jrs,jsc->jrc/dot_general | solution.py:66
  114.6 1.5 collective-permute-start.1
  116.6 1.9 fusion.9
  118.6 43.1 %collective-permute-done.1 = f32[2,256,1024]{1,2,0:T(8,128)S(1)} collective-permute-done((f32[2,256,1024]{1,2,0:T(8,128)S(1)}, f32[2,256,1024]{1,2,0:T(8,128)S(1)}, u32[]{:S(2)}, u32[]{:S(2)}) %collective-permute-start.1) | collective-permute-done | bytes 2097184 | tf_op jit(solution)/shard_map/ppermute | solution.py:14
  161.6 2.1 bitcast_add_fusion.3
  163.7 2.8 collective-permute-start.2
  167.0 1.9 fusion.6
  169.0 42.1 %collective-permute-done.2 = f32[2,256,1024]{1,2,0:T(8,128)S(1)} collective-permute-done((f32[2,256,1024]{1,2,0:T(8,128)S(1)}, f32[2,256,1024]{1,2,0:T(8,128)S(1)}, u32[]{:S(2)}, u32[]{:S(2)}) %collective-permute-start.2) | collective-permute-done | bytes 2097184 | tf_op jit(solution)/shard_map/ppermute | solution.py:14
  211.1 2.0 bitcast_add_fusion.2
  213.1 1.6 collective-permute-start.3
  214.7 0.5 fusion.1
  215.6 2.0 fusion.3
  217.6 40.6 %collective-permute-done.3 = f32[2,256,1024]{1,2,0:T(8,128)S(1)} collective-permute-done((f32[2,256,1024]{1,2,0:T(8,128)S(1)}, f32[2,256,1024]{1,2,0:T(8,128)S(1)}, u32[]{:S(2)}, u32[]{:S(2)}) %collective-permute-start.3) | collective-permute-done | bytes 2097184 | tf_op jit(solution)/shard_map/ppermute | solution.py:14
  258.3 3.5 %fusion.14 = f32[2,256,1024]{2,1,0:T(8,128)S(1)} fusion(f32[2,256,1024]{1,2,0:T(8,128)S(1)} %collective-permute-done.3, f32[2,256,256]{1,0,2:T(2,128)S(1)} %bitcast.71), kind=kOutput, calls=%fused_computation.26 | convolution fusion | flops 1610612736 | bytes 4718592 | tf_op jit(solution)/shard_map/jrs,jsc->jrc/dot_general | solution.py:66
  261.8 5.1 %fusion = f32[2,1024,512]{1,2,0:T(8,128)} fusion(f32[2,512,256]{2,1,0:T(8,128)S(1)} %copy-done, f32[2,256,1024]{2,1,0:T(8,128)S(1)} %fusion.14, f32[2,1024,256]{1,2,0:T(8,128)S(1)} %fusion.3), kind=kOutput, calls=%fused_computation.1 | convolution fusion | flops 3221749760 | bytes 9437184 | tf_op jit(solution)/shard_map/jlr,jrc->cjl/dot_general | solution.py:75
  266.9 5.4 %copy.22 = f32[1024,1024]{1,0:T(8,128)} copy(f32[1024,1024]{0,1:T(8,128)} %bitcast.66) | data formatting | bytes 8388608 | tf_op jit(solution)/shard_map/reshape | solution.py:83
  272.3 53.1 %reduce-scatter.2.cloned.1.call-done = f32[256,1024]{1,0:T(8,128)} async-done(((f32[1024,1024]{1,0:T(8,128)}), f32[256,1024]{1,0:T(8,128)}) %reduce-scatter.2.cloned.1.call-update) | async-done | bytes 1048592 | tf_op jit(solution)/shard_map/reduce_scatter | solution.py:82
  (16 shorter events, 1.9 us)
Async XLA Ops:
  6.5 255.2 %copy-start = (f32[2,512,256]{2,1,0:T(8,128)S(1)}, f32[2,512,256]{2,1,0:T(8,128)}, u32[]{:S(2)}) copy-start(f32[2,512,256]{2,1,0:T(8,128)} %param.9) | copy-start | bytes 3145732
  6.5 97.2 %all-gather.2.cloned.1.call-start = ((), (), s32[]{:S(2)}) async-start(), calls=%async_computation.1 | async-start | bytes 10485760 | tf_op jit(solution)/shard_map/all_gather | solution.py:37
  14.1 92.6 %copy-start.2 = (s32[4,256]{1,0:T(4,128)S(1)}, s32[4,256]{1,0:T(4,128)}, u32[]{:S(2)}) copy-start(s32[4,256]{1,0:T(4,128)} %param.11) | copy-start | bytes 12292
  14.1 311.3 %reduce-scatter.2.cloned.1.call-start = ((), (), s32[]{:S(2)}) async-start(), calls=%async_computation.2 | async-start | bytes 5242880 | tf_op jit(solution)/shard_map/reduce_scatter | solution.py:82
  103.7 3.0 copy-start.1
  105.8 5.3 %collective-permute-start = (f32[2,256,1024]{2,1,0:T(8,128)S(1)}, f32[2,256,1024]{2,1,0:T(8,128)S(1)}, u32[]{:S(2)}, u32[]{:S(2)}) collective-permute-start(f32[2,256,1024]{2,1,0:T(8,128)S(1)} %bitcast.68), channel_id=1, source_target_pairs={{0,1},{1,0},{2,3},{3,2},{4,5},{5,4},{6,7},{7,6},{8,9},{9,8},{10,11... | collective-permute-start | bytes 6291464 | tf_op jit(solution)/shard_map/ppermute | solution.py:14
  114.6 47.0 %collective-permute-start.1 = (f32[2,256,1024]{1,2,0:T(8,128)S(1)}, f32[2,256,1024]{1,2,0:T(8,128)S(1)}, u32[]{:S(2)}, u32[]{:S(2)}) collective-permute-start(f32[2,256,1024]{1,2,0:T(8,128)S(1)} %bitcast_add_fusion.4), channel_id=1, source_target_pairs={{0,2},{2,0},{1,3},{3,1},{4,6},{6,4},{5,7},{7,5},{8,10},{10,8},{9,1... | collective-permute-start | bytes 6291464 | tf_op jit(solution)/shard_map/ppermute | solution.py:14
  163.7 47.3 %collective-permute-start.2 = (f32[2,256,1024]{1,2,0:T(8,128)S(1)}, f32[2,256,1024]{1,2,0:T(8,128)S(1)}, u32[]{:S(2)}, u32[]{:S(2)}) collective-permute-start(f32[2,256,1024]{1,2,0:T(8,128)S(1)} %bitcast_add_fusion.3), channel_id=1, source_target_pairs={{0,4},{4,0},{1,5},{5,1},{2,6},{6,2},{3,7},{7,3},{8,12},{12,8},{9,1... | collective-permute-start | bytes 6291464 | tf_op jit(solution)/shard_map/ppermute | solution.py:14
  213.1 45.2 %collective-permute-start.3 = (f32[2,256,1024]{1,2,0:T(8,128)S(1)}, f32[2,256,1024]{1,2,0:T(8,128)S(1)}, u32[]{:S(2)}, u32[]{:S(2)}) collective-permute-start(f32[2,256,1024]{1,2,0:T(8,128)S(1)} %bitcast_add_fusion.2), channel_id=1, source_target_pairs={{0,8},{8,0},{1,9},{9,1},{2,10},{10,2},{3,11},{11,3},{4,12},{12,4},... | collective-permute-start | bytes 6291464 | tf_op jit(solution)/shard_map/ppermute | solution.py:14
Sparse Core Ops, SparseCore 0:
  14.2 89.4 all-gather.1
  272.4 52.9 reduce-scatter.1
where the time goes:
time: 332 us
  waiting for transfers between devices  267 us (80%)
  matrix products  35 us (11%)
  between operations  14.2 us (4%)
  local copies, waits for them, and re-layouts  7.52 us (2%)
  starting transfers between devices  6.95 us (2%)
    ppermute x4, waiting for transfers between devices, swapped(): return lax.ppermute(block, axis, route)  126 us
    all_gather x1, waiting for transfers between devices, body(): shards = lax.all_gather(flattened, 'obs', axis=0, tiled=True)  87.6 us
    reduce_scatter x1, waiting for transfers between devices, body(): lax.psum_scatter(product.reshape(share_cols * lax.axis_size('obs'), node_...  53.1 us
    dot_general x4, matrix products, body(): jnp.einsum('jrs,jsc->jrc', far_part, partner, precision=highest_level, pr...  11.1 us
    dot_general x4, matrix products, body(): jnp.einsum('jrs,jsc->jrc', own_part, carried, precision=highest_level, pr...  9.3 us
    dot_general x1, matrix products, body(): jnp.einsum('jlr,jlc->jrc', observer_leaf_bases, block_list, precision=hig...  7.56 us
    ppermute x4, starting transfers between devices, swapped(): return lax.ppermute(block, axis, route)  6.9 us
  transfers between devices with their start and end apart: 6, of which 5 were waited for; matrix products, arithmetic and copies ran while one was open for 4% of the time, Pallas kernels for 0%

commit v1 on v0

--- a/solution.py
+++ b/solution.py
@@ -34,7 +34,9 @@
     block_rows = node_count * rank_size
     flattened = projected_field.reshape(block_rows, col_count)
     target = source * block_rows
-    shards = lax.all_gather(flattened, "obs", axis=0, tiled=True)
+    shards = jnp.concatenate(
+        lax.all_to_all(jnp.stack([flattened] * lax.axis_size("obs")), "obs", 0, 0), axis=0
+    )
     first_row = jnp.int32(0)
     row_count = shards.shape[0]
     offset = jnp.clip(target, 0, row_count - block_rows)

time: 332 us -> 346 us (1.042)
  starting transfers between devices: 6.95 us -> 16.2 us
  local copies, waits for them, and re-layouts: 7.52 us -> 11.8 us
    all_to_all x0 -> x1, waiting for transfers between devices: none -> 89.8 us  [body(): lax.all_to_all(jnp.stack([flattened] * lax.axis_size('obs')), 'obs', 0, 0)]
    all_gather x1 -> x0, waiting for transfers between devices: 87.6 us -> none  [body(): shards = lax.all_gather(flattened, 'obs', axis=0, tiled=True)]
    all_to_all x0 -> x1, starting transfers between devices: none -> 5.76 us  [body(): lax.all_to_all(jnp.stack([flattened] * lax.axis_size('obs')), 'obs', 0, 0)]
    another operation x0 -> x1, local copies, waits for them, and re-layouts: none -> 4.3 us  [body(): jnp.stack([flattened] * lax.axis_size('obs'))]
    ppermute x4, starting transfers between devices: 6.9 us -> 10.4 us  [swapped(): return lax.ppermute(block, axis, route)]
where the time goes in v1:
time: 346 us
  waiting for transfers between devices  268 us (77%)
  matrix products  33.9 us (10%)
  starting transfers between devices  16.2 us (5%)
  between operations  14.2 us (4%)
  local copies, waits for them, and re-layouts  11.8 us (3%)
    ppermute x4, waiting for transfers between devices, swapped(): return lax.ppermute(block, axis, route)  125 us
    all_to_all x1, waiting for transfers between devices, body(): lax.all_to_all(jnp.stack([flattened] * lax.axis_size('obs')), 'obs', 0, 0)  89.8 us
    reduce_scatter x1, waiting for transfers between devices, body(): lax.psum_scatter(product.reshape(share_cols * lax.axis_size('obs'), node_...  53 us
    dot_general x4, matrix products, body(): jnp.einsum('jrs,jsc->jrc', far_part, partner, precision=highest_level, pr...  11.1 us
    ppermute x4, starting transfers between devices, swapped(): return lax.ppermute(block, axis, route)  10.4 us
    dot_general x4, matrix products, body(): jnp.einsum('jrs,jsc->jrc', own_part, carried, precision=highest_level, pr...  9.44 us
  transfers between devices with their start and end apart: 6, of which 5 were waited for; matrix products, arithmetic and copies ran while one was open for 4% of the time, Pallas kernels for 0%

profile of v1, /device:TPU:1, one launch (start us, length us, event | category | flops | bytes accessed | tf_op | source)
XLA Modules:
  0.0 345.9 jit_solution(9526779768448589648)
XLA Ops:
  6.5 6.4 %fusion.30 = f32[2,256,1024]{2,1,0:T(8,128)S(1)} fusion(f32[2,512,256]{2,1,0:T(8,128)} %param.7, f32[2,512,1024]{2,1,0:T(8,128)} %bitcast.71), kind=kOutput, calls=%fused_computation.43 | convolution fusion | flops 3221225472 | bytes 7340032 | tf_op jit(solution)/shard_map/jlr,jlc->jrc/dot_general | solution.py:26
  13.0 4.3 %stack.3 = f32[4,512,1024]{2,1,0:T(8,128)} broadcast(f32[512,1024]{1,0:T(8,128)S(1)} %bitcast.68), dimensions={1,2} | broadcast | bytes 10485760 | tf_op jit(solution)/shard_map/stack | solution.py:38
  17.3 5.8 %all-to-all-start = ((f32[4,512,1024]{2,1,0:T(8,128)}), f32[4,512,1024]{2,1,0:T(8,128)}, u32[]{:S(2)}, u32[]{:S(2)}) async-start(f32[4,512,1024]{2,1,0:T(8,128)} %stack.3), calls=%async_computation | async-start | bytes 16777216 | tf_op jit(solution)/shard_map/all_to_all | solution.py:38
  23.1 1.3 dynamic_slice.6
  25.0 89.8 %all-to-all-done = f32[4,512,1024]{2,1,0:T(8,128)} async-done(((f32[4,512,1024]{2,1,0:T(8,128)}), f32[4,512,1024]{2,1,0:T(8,128)}, u32[]{:S(2)}, u32[]{:S(2)}) %all-to-all-start) | async-done | bytes 8388640 | tf_op jit(solution)/shard_map/all_to_all | solution.py:38
  114.8 2.0 dynamic-slice_select_fusion
  116.9 3.6 %collective-permute-start = (f32[2,256,1024]{2,1,0:T(8,128)S(1)}, f32[2,256,1024]{2,1,0:T(8,128)S(1)}, u32[]{:S(2)}, u32[]{:S(2)}) collective-permute-start(f32[2,256,1024]{2,1,0:T(8,128)S(1)} %bitcast.69), channel_id=1, source_target_pairs={{0,1},{1,0},{2,3},{3,2},{4,5},{5,4},{6,7},{7,6},{8,9},{9,8},{10,11... | collective-permute-start | bytes 6291464 | tf_op jit(solution)/shard_map/ppermute | solution.py:14
  121.4 3.5 fusion.12
  124.9 3.5 %bitcast_add_fusion.4 = f32[2,256,1024]{1,2,0:T(8,128)S(1)} fusion(f32[2,1024,256]{2,1,0:T(8,128)S(1)} %fusion.12, f32[2,256,256]{2,1,0:T(8,128)S(1)} %convolution_bitcast_fusion.2, f32[2,256,1024]{2,1,0:T(8,128)S(1)} %collective-permute-done), kind=kOutput, calls=%fused_computation.4 | convolution fusion | flops 1611137024 | bytes 6815744 | tf_op jit(solution)/shard_map/jrs,jsc->jrc/dot_general | solution.py:68
  128.4 1.8 collective-permute-start.1
  130.7 2.0 fusion.9
  132.7 42.6 %collective-permute-done.1 = f32[2,256,1024]{1,2,0:T(8,128)S(1)} collective-permute-done((f32[2,256,1024]{1,2,0:T(8,128)S(1)}, f32[2,256,1024]{1,2,0:T(8,128)S(1)}, u32[]{:S(2)}, u32[]{:S(2)}) %collective-permute-start.1) | collective-permute-done | bytes 2097184 | tf_op jit(solution)/shard_map/ppermute | solution.py:14
  175.3 2.1 bitcast_add_fusion.3
  177.4 3.1 collective-permute-start.2
  180.9 2.0 fusion.6
  182.9 41.7 %collective-permute-done.2 = f32[2,256,1024]{1,2,0:T(8,128)S(1)} collective-permute-done((f32[2,256,1024]{1,2,0:T(8,128)S(1)}, f32[2,256,1024]{1,2,0:T(8,128)S(1)}, u32[]{:S(2)}, u32[]{:S(2)}) %collective-permute-start.2) | collective-permute-done | bytes 2097184 | tf_op jit(solution)/shard_map/ppermute | solution.py:14
  224.6 2.1 bitcast_add_fusion.2
  226.7 1.9 collective-permute-start.3
  229.5 2.0 fusion.3
  231.5 40.5 %collective-permute-done.3 = f32[2,256,1024]{1,2,0:T(8,128)S(1)} collective-permute-done((f32[2,256,1024]{1,2,0:T(8,128)S(1)}, f32[2,256,1024]{1,2,0:T(8,128)S(1)}, u32[]{:S(2)}, u32[]{:S(2)}) %collective-permute-start.3) | collective-permute-done | bytes 2097184 | tf_op jit(solution)/shard_map/ppermute | solution.py:14
  272.0 3.5 %fusion.14 = f32[2,256,1024]{2,1,0:T(8,128)S(1)} fusion(f32[2,256,1024]{1,2,0:T(8,128)S(1)} %collective-permute-done.3, f32[2,256,256]{1,0,2:T(2,128)S(1)} %bitcast.72), kind=kOutput, calls=%fused_computation.26 | convolution fusion | flops 1610612736 | bytes 4718592 | tf_op jit(solution)/shard_map/jrs,jsc->jrc/dot_general | solution.py:68
  275.4 5.1 %fusion = f32[2,1024,512]{1,2,0:T(8,128)} fusion(f32[2,512,256]{2,1,0:T(8,128)S(1)} %copy-done, f32[2,256,1024]{2,1,0:T(8,128)S(1)} %fusion.14, f32[2,1024,256]{1,2,0:T(8,128)S(1)} %fusion.3), kind=kOutput, calls=%fused_computation.1 | convolution fusion | flops 3221749760 | bytes 9437184 | tf_op jit(solution)/shard_map/jlr,jrc->cjl/dot_general | solution.py:77
  280.6 5.4 %copy.22 = f32[1024,1024]{1,0:T(8,128)} copy(f32[1024,1024]{0,1:T(8,128)} %bitcast.67) | data formatting | bytes 8388608 | tf_op jit(solution)/shard_map/reshape | solution.py:85
  286.0 53.0 %reduce-scatter.2.cloned.1.call-done = f32[256,1024]{1,0:T(8,128)} async-done(((f32[1024,1024]{1,0:T(8,128)}), f32[256,1024]{1,0:T(8,128)}) %reduce-scatter.2.cloned.1.call-update) | async-done | bytes 1048592 | tf_op jit(solution)/shard_map/reduce_scatter | solution.py:84
  (16 shorter events, 2.8 us)
Async XLA Ops:
  6.5 268.9 %copy-start = (f32[2,512,256]{2,1,0:T(8,128)S(1)}, f32[2,512,256]{2,1,0:T(8,128)}, u32[]{:S(2)}) copy-start(f32[2,512,256]{2,1,0:T(8,128)} %param.9) | copy-start | bytes 3145732
  17.3 103.2 %copy-start.2 = (s32[4,256]{1,0:T(4,128)S(1)}, s32[4,256]{1,0:T(4,128)}, u32[]{:S(2)}) copy-start(s32[4,256]{1,0:T(4,128)} %param.11) | copy-start | bytes 12292
  17.3 97.6 %all-to-all-start = ((f32[4,512,1024]{2,1,0:T(8,128)}), f32[4,512,1024]{2,1,0:T(8,128)}, u32[]{:S(2)}, u32[]{:S(2)}) async-start(f32[4,512,1024]{2,1,0:T(8,128)} %stack.3), calls=%async_computation | async-start | bytes 16777216 | tf_op jit(solution)/shard_map/all_to_all | solution.py:38
  23.0 316.0 %reduce-scatter.2.cloned.1.call-start = ((), (), s32[]{:S(2)}) async-start(), calls=%async_computation.2 | async-start | bytes 5242880 | tf_op jit(solution)/shard_map/reduce_scatter | solution.py:84
  114.8 5.7 %copy-start.1 = (f32[4,2,256,512]{3,2,1,0:T(8,128)S(1)}, f32[4,2,256,512]{3,2,1,0:T(8,128)}, u32[]{:S(2)}) copy-start(f32[4,2,256,512]{3,2,1,0:T(8,128)} %param.8) | copy-start | bytes 12582916
  116.9 8.0 %collective-permute-start = (f32[2,256,1024]{2,1,0:T(8,128)S(1)}, f32[2,256,1024]{2,1,0:T(8,128)S(1)}, u32[]{:S(2)}, u32[]{:S(2)}) collective-permute-start(f32[2,256,1024]{2,1,0:T(8,128)S(1)} %bitcast.69), channel_id=1, source_target_pairs={{0,1},{1,0},{2,3},{3,2},{4,5},{5,4},{6,7},{7,6},{8,9},{9,8},{10,11... | collective-permute-start | bytes 6291464 | tf_op jit(solution)/shard_map/ppermute | solution.py:14
  128.4 46.9 %collective-permute-start.1 = (f32[2,256,1024]{1,2,0:T(8,128)S(1)}, f32[2,256,1024]{1,2,0:T(8,128)S(1)}, u32[]{:S(2)}, u32[]{:S(2)}) collective-permute-start(f32[2,256,1024]{1,2,0:T(8,128)S(1)} %bitcast_add_fusion.4), channel_id=1, source_target_pairs={{0,2},{2,0},{1,3},{3,1},{4,6},{6,4},{5,7},{7,5},{8,10},{10,8},{9,1... | collective-permute-start | bytes 6291464 | tf_op jit(solution)/shard_map/ppermute | solution.py:14
  177.4 47.3 %collective-permute-start.2 = (f32[2,256,1024]{1,2,0:T(8,128)S(1)}, f32[2,256,1024]{1,2,0:T(8,128)S(1)}, u32[]{:S(2)}, u32[]{:S(2)}) collective-permute-start(f32[2,256,1024]{1,2,0:T(8,128)S(1)} %bitcast_add_fusion.3), channel_id=1, source_target_pairs={{0,4},{4,0},{1,5},{5,1},{2,6},{6,2},{3,7},{7,3},{8,12},{12,8},{9,1... | collective-permute-start | bytes 6291464 | tf_op jit(solution)/shard_map/ppermute | solution.py:14
  226.7 45.2 %collective-permute-start.3 = (f32[2,256,1024]{1,2,0:T(8,128)S(1)}, f32[2,256,1024]{1,2,0:T(8,128)S(1)}, u32[]{:S(2)}, u32[]{:S(2)}) collective-permute-start(f32[2,256,1024]{1,2,0:T(8,128)S(1)} %bitcast_add_fusion.2), channel_id=1, source_target_pairs={{0,8},{8,0},{1,9},{9,1},{2,10},{10,2},{3,11},{11,3},{4,12},{12,4},... | collective-permute-start | bytes 6291464 | tf_op jit(solution)/shard_map/ppermute | solution.py:14
Sparse Core Ops, SparseCore 0:
  286.1 52.8 reduce-scatter.1
